TPU v7x, 32 devices: a whole 2x2x4 slice. The times are simulated.
32 devices in a mesh: dp: 4 (over z), group: 8 (over y, x, core).
Axes of the slice: x: 2, y: 2, z: 4, core: 2. Of those that a mesh axis runs over, the one named last changes fastest.
Arguments:
- query: bfloat16 [4096, 4096], P(('dp', 'group')), may hold values from -6 to 6
- comp_key: bfloat16 [4096, 512], P(('dp', 'group')), may hold values from -6 to 6
- comp_value: bfloat16 [4096, 512], P(('dp', 'group')), may hold values from -6 to 6
- prompt_key: bfloat16 [128, 512], P(('dp', 'group')), may hold values from -6 to 6
- prompt_value: bfloat16 [128, 512], P(('dp', 'group')), may hold values from -6 to 6
- d_out: bfloat16 [4096, 4096], P(('dp', 'group')), may hold values from -6 to 6
- q_gain: float32 [128], replicated, may hold values from 0.5 to 1.5
- k_gain: float32 [128], replicated, may hold values from 0.5 to 1.5
- lengths: int32 [32], P(('dp', 'group')), may hold values from 1 to 128, 2560 in all
Outputs:
- d_query: bfloat16 [4096, 4096], P(('dp', 'group'))
- d_comp_key: bfloat16 [4096, 512], P(('dp', 'group'))
- d_comp_value: bfloat16 [4096, 512], P(('dp', 'group'))
- d_prompt_key: bfloat16 [128, 512], P(('dp', 'group'))
- d_prompt_value: bfloat16 [128, 512], P(('dp', 'group'))
- d_q_gain: float32 [128], replicated
- d_k_gain: float32 [128], replicated
Inputs may be any that keep to these rules, and one draw needn't show every extreme that they name: `lengths`: each entry is the live slots of one completion, at most 128; some completion has exactly 128.
All inputs are finite; a program needn't handle non-finite values. No bound on the sum of `lengths` on one device may be relied on, other than what follows from the above.
Results may differ from a plain program's by a relative error of at most 0.025.
Values may be sent and summed in bfloat16 or wider, within the bound.
A program may use at most 64 MiB of HBM per device.

v0:
```python
import jax
import jax.numpy as jnp
from jax import lax
from jax.sharding import PartitionSpec as P

HD = 128
HQ = 32
HK = 4


EPS = 1e-06


def normalize(vectors, gain):
    wide = vectors.astype(jnp.float32)
    inverse = lax.rsqrt(jnp.mean(wide * wide, axis=-1, keepdims=True) + EPS)
    unit = wide * inverse
    return ((unit * gain).astype(jnp.bfloat16), unit, inverse)


def norm_back(grad, unit, inverse, gain):
    scaled = grad * gain
    back = inverse * (scaled - unit * jnp.mean(scaled * unit, axis=-1, keepdims=True))
    return (back, jnp.sum((grad * unit).reshape(-1, unit.shape[-1]), axis=0))


def head_grads(query_head, key_head, value_head, grad_head, visible, scale):
    scores = (
        jnp.einsum("cgd,kd->gck", query_head, key_head, preferred_element_type=jnp.float32) * scale
    )
    expo = jnp.where(visible[None], jnp.exp(scores), 0.0)
    totals = jnp.sum(expo, axis=-1, keepdims=True)
    rounded = (expo / totals).astype(jnp.bfloat16)
    output = jnp.einsum("gck,kd->cgd", rounded, value_head, preferred_element_type=jnp.float32)
    delta = jnp.transpose(jnp.sum(grad_head.astype(jnp.float32) * output, axis=-1))[..., None]
    dprob = jnp.einsum("cgd,kd->gck", grad_head, value_head, preferred_element_type=jnp.float32)
    dscore = (expo / totals * (dprob - delta)).astype(jnp.bfloat16)
    dquery = jnp.einsum("gck,kd->cgd", dscore, key_head, preferred_element_type=jnp.float32) * scale
    dkey = jnp.einsum("gck,cgd->kd", dscore, query_head, preferred_element_type=jnp.float32) * scale
    dvalue = jnp.einsum("gck,cgd->kd", rounded, grad_head, preferred_element_type=jnp.float32)
    return (dquery, dkey, dvalue, totals, delta)


def local(query, comp_key, comp_value, prompt_key, prompt_value, d_out, q_gain, k_gain, lengths):
    count = query.shape[0]
    shard = prompt_key.shape[0]
    groups = HQ // HK
    scale = HD ** (-0.5)
    qnorm, qunit, qinv = normalize(query.reshape(count, HQ, HD), q_gain)
    cnorm, cunit, cinv = normalize(comp_key.reshape(count, HK, HD), k_gain)
    pnorm, punit, pinv = normalize(prompt_key.reshape(shard, HK, HD), k_gain)
    pkeys, pvalues = (
        lax.all_gather(pnorm.reshape(shard, HK * HD), "group", axis=0, tiled=True),
        lax.all_gather(prompt_value, "group", axis=0, tiled=True),
    )
    prompt_len = pkeys.shape[0]
    keys = jnp.concatenate([pkeys, cnorm.reshape(count, HK * HD)], axis=0).reshape(-1, HK, HD)
    values = jnp.concatenate([pvalues, comp_value], axis=0).reshape(-1, HK, HD)
    slots = lax.broadcasted_iota(jnp.int32, (count, count), 0)
    others = lax.broadcasted_iota(jnp.int32, (count, count), 1)
    visible = jnp.concatenate([jnp.ones((count, prompt_len), bool), others <= slots], axis=1)
    live = (jnp.arange(count, dtype=jnp.int32) < lengths[0])[:, None]
    masked = jnp.where(live, d_out, jnp.zeros_like(d_out))
    query_four = qnorm.reshape(count, HK, groups, HD)
    grad_four = masked.reshape(count, HK, groups, HD)
    results = [
        head_grads(
            query_four[:, head], keys[:, head], values[:, head], grad_four[:, head], visible, scale
        )
        for head in range(HK)
    ]
    dquery = jnp.stack([item[0] for item in results], axis=1).reshape(count, HQ, HD)
    dkey_all = jnp.stack([item[1] for item in results], axis=1)
    dvalue_all = jnp.stack([item[2] for item in results], axis=1)
    term = jnp.concatenate(
        [
            dkey_all[:prompt_len].reshape(prompt_len, HK * HD),
            dvalue_all[:prompt_len].reshape(prompt_len, HK * HD),
        ],
        axis=1,
    )
    summed = lax.psum_scatter(
        term.astype(jnp.bfloat16), "group", scatter_dimension=0, tiled=True
    ).astype(jnp.float32)
    dkey_comp = dkey_all[prompt_len:]
    dvalue_comp = dvalue_all[prompt_len:]
    dkey_prompt = summed[:, : HK * HD].reshape(shard, HK, HD)
    dvalue_prompt = summed[:, HK * HD :]
    dq, gain_query = norm_back(dquery, qunit, qinv, q_gain)
    dck, gain_comp = norm_back(dkey_comp, cunit, cinv, k_gain)
    dpk, gain_prompt = norm_back(dkey_prompt, punit, pinv, k_gain)
    gain_query, gain_key = lax.psum((gain_query, gain_comp + gain_prompt), ("dp", "group"))
    return (
        dq.reshape(count, HQ * HD).astype(jnp.bfloat16),
        dck.reshape(count, HK * HD).astype(jnp.bfloat16),
        dvalue_comp.reshape(count, HK * HD).astype(jnp.bfloat16),
        dpk.reshape(shard, HK * HD).astype(jnp.bfloat16),
        dvalue_prompt.astype(jnp.bfloat16),
        gain_query,
        gain_key,
    )


def solution(mesh):
    return jax.shard_map(
        local,
        mesh=mesh,
        in_specs=(
            P(("dp", "group"), None),
            P(("dp", "group"), None),
            P(("dp", "group"), None),
            P(("dp", "group"), None),
            P(("dp", "group"), None),
            P(("dp", "group"), None),
            P(),
            P(),
            P(("dp", "group")),
        ),
        out_specs=(
            P(("dp", "group"), None),
            P(("dp", "group"), None),
            P(("dp", "group"), None),
            P(("dp", "group"), None),
            P(("dp", "group"), None),
            P(),
            P(),
        ),
        check_vma=False,
    )
```

profile of v0, /device:TPU:0, one launch (start us, length us, event | category | flops | bytes accessed | tf_op | source)
XLA Modules:
  0.0 174.6 jit_solution(7659037354188881462)
XLA Ops:
  7.2 0.6 iota_compare_fusion
  7.8 0.7 broadcast_bitcast_fusion.3
  8.5 0.7 reshape.176
  9.4 0.4 copy-done.30
  9.9 0.6 copy-done.32
  10.5 0.7 fusion.87
  11.2 10.6 %all-gather = bf16[8,4,512]{2,1,0:T(4,128)(2,1)S(1)} all-gather(bf16[1,4,512]{2,1,0:T(4,128)(2,1)S(1)} %fusion.87), channel_id=1, replica_groups=mesh['dp'=4,'group'=8] {'group'}, dimensions={0}, use_global_device_ids=true | all-gather | bytes 36864 | tf_op jit(solution)/shard_map/all_gather | solution.py:53
  21.8 0.6 copy.94
  22.4 1.0 copy.92
  23.8 0.7 copy.91
  24.7 0.8 add_rsqrt_fusion
  25.4 0.5 copy.96
  26.0 1.3 concatenate.21
  27.3 1.3 fusion.81
  28.6 1.4 multiply_convert_fusion
  30.0 2.0 %fusion.52 = f32[8,128,160]{1,2,0:T(8,128)} fusion(pred[128,160]{0,1:T(8,128)(4,1)} %concatenate.21, bf16[128,4,8,128]{3,0,2,1:T(8,128)(2,1)S(1)} %multiply_convert_fusion, bf16[128,4,128]{2,0,1:T(8,128)(2,1)S(1)} %copy.95, bf16[32,4,128]{2,0,1:T(8,128)(2,1)} %copy.94), kind=kOutput, calls=%fused_computation.88 | convolution fusion | flops 42517664 | bytes 1101824 | tf_op jit(solution)/shard_map/div | solution.py:37
  32.0 1.9 %fusion.54 = f32[8,128,160]{1,2,0:T(8,128)} fusion(pred[128,160]{0,1:T(8,128)(4,1)} %concatenate.21, bf16[128,4,8,128]{3,0,2,1:T(8,128)(2,1)S(1)} %multiply_convert_fusion, bf16[128,4,128]{2,0,1:T(8,128)(2,1)S(1)} %copy.95, bf16[32,4,128]{2,0,1:T(8,128)(2,1)} %copy.94), kind=kOutput, calls=%fused_computation.90 | convolution fusion | flops 42517664 | bytes 1101824 | tf_op jit(solution)/shard_map/div | solution.py:37
  33.9 2.0 %fusion.56 = f32[8,128,160]{1,2,0:T(8,128)} fusion(pred[128,160]{0,1:T(8,128)(4,1)} %concatenate.21, bf16[128,4,8,128]{3,0,2,1:T(8,128)(2,1)S(1)} %multiply_convert_fusion, bf16[128,4,128]{2,0,1:T(8,128)(2,1)S(1)} %copy.95, bf16[32,4,128]{2,0,1:T(8,128)(2,1)} %copy.94), kind=kOutput, calls=%fused_computation.92 | convolution fusion | flops 42517664 | bytes 1101824 | tf_op jit(solution)/shard_map/div | solution.py:37
  36.5 0.5 iota_compare_fusion.1
  37.1 9.3 %all-gather.1 = bf16[8,4,512]{2,1,0:T(4,128)(2,1)S(1)} all-gather(bf16[1,4,512]{2,1,0:T(4,128)(2,1)} %bitcast.375), channel_id=1, replica_groups=mesh['dp'=4,'group'=8] {'group'}, dimensions={0}, use_global_device_ids=true | all-gather | bytes 36864 | tf_op jit(solution)/shard_map/all_gather | solution.py:54
  46.3 0.9 pad_maximum_fusion.2
  47.3 0.9 fusion.122
  48.2 2.3 %copy.98 = bf16[128,4096]{0,1:T(8,128)(2,1)} copy(bf16[128,4096]{1,0:T(8,128)(2,1)} %param.14) | data formatting | bytes 2097152 | tf_op args[5]
  50.5 1.3 broadcast_select_fusion
  51.8 1.0 fusion.121
  52.8 1.8 %copy.133 = bf16[128,1,8,128]{3,0,2,1:T(8,128)(2,1)} copy(bf16[128,1,8,128]{0,3,2,1:T(8,128)(2,1)} %get-tuple-element.38) | data formatting | bytes 524288
  54.6 1.8 %copy.137 = bf16[128,1,8,128]{3,0,2,1:T(8,128)(2,1)} copy(bf16[128,1,8,128]{0,3,2,1:T(8,128)(2,1)} %get-tuple-element.39) | data formatting | bytes 524288
  56.4 1.8 %copy.135 = bf16[128,1,8,128]{3,0,2,1:T(8,128)(2,1)} copy(bf16[128,1,8,128]{0,3,2,1:T(8,128)(2,1)} %get-tuple-element.40) | data formatting | bytes 524288
  58.2 1.8 %copy.139 = bf16[128,1,8,128]{3,0,2,1:T(8,128)(2,1)} copy(bf16[128,1,8,128]{0,3,2,1:T(8,128)(2,1)} %get-tuple-element.41) | data formatting | bytes 524288
  60.0 2.1 %fusion.50 = f32[8,128,160]{1,2,0:T(8,128)} fusion(bf16[160,128,1]{1,0,2:T(8,128)(2,1)} %fusion.81, pred[128,160]{0,1:T(8,128)(4,1)} %concatenate.21, bf16[128,4,8,128]{3,0,2,1:T(8,128)(2,1)} %copy-done.6), kind=kOutput, calls=%fused_computation.86 | convolution fusion | flops 42435744 | bytes 978944 | tf_op jit(solution)/shard_map/div | solution.py:37
  62.1 1.5 convolution_bitcast_fusion.8
  63.6 1.7 fusion.37
  65.3 1.1 fusion.36
  66.7 0.3 convolution_bitcast_fusion.9
  67.0 0.5 fusion.38
  67.5 0.2 fusion.35
  67.8 0.2 fusion.44
  68.1 0.3 convolution_bitcast_fusion.10
  68.4 0.5 fusion.39
  68.9 0.2 fusion.34
  69.1 0.2 fusion.46
  69.4 0.2 convolution_bitcast_fusion.11
  69.7 0.5 fusion.40
  70.2 0.2 fusion.33
  70.8 0.4 copy-done.12
  71.2 0.6 pad_maximum_fusion.3
  71.9 1.3 broadcast_bitcast_fusion
  73.2 2.1 %fusion.29 = f32[128,1,8,128]{3,0,2,1:T(8,128)} fusion(bf16[160,128,1]{1,0,2:T(8,128)(2,1)} %fusion.81, bf16[8,128,160]{1,2,0:T(8,128)(2,1)} %copy-done.8), kind=kOutput, calls=%fused_computation.51 | convolution fusion | flops 42074112 | bytes 892928 | tf_op jit(solution)/shard_map/gck,kd->cgd/dot_general | solution.py:38
  75.3 2.2 %fusion.30 = f32[128,1,8,128]{3,0,2,1:T(8,128)} fusion(bf16[8,128,160]{1,2,0:T(8,128)(2,1)} %copy-done.9, bf16[128,4,128]{2,0,1:T(8,128)(2,1)S(1)} %copy.95, bf16[32,4,128]{2,0,1:T(8,128)(2,1)} %copy.94), kind=kOutput, calls=%fused_computation.53 | convolution fusion | flops 42156032 | bytes 1015808 | tf_op jit(solution)/shard_map/gck,kd->cgd/dot_general | solution.py:38
  77.5 1.2 fusion.31
  78.7 0.7 maximum_convert_fusion
  79.4 1.1 fusion.32
  80.7 0.3 multiply_reduce_fusion.1
  81.2 3.6 %multiply_reduce_fusion = (f32[128,4,8]{0,2,1:T(8,128)S(1)}, f32[128,4,8,128]{3,0,2,1:T(8,128)}) fusion(f32[128,4,8,128]{3,0,2,1:T(8,128)S(1)} %copy.96, f32[128]{0:T(128)S(1)} %copy-done.45, f32[128,4,8]{0,2,1:T(8,128)S(1)} %get-tuple-element.49, f32[128,1,8,128]{3,0,2,1:T(8,128)} %fusion.29, f32[128,1,8,128]{3,0,2,1:T(8,128)} %fusion.30, ...), kind=kLoop, calls=%fused_computation.11 | loop fusion | flops 3665920 | bytes 6324736 | tf_op jit(solution)/shard_map/reduce_sum | solution.py:23
  84.8 2.0 %copy.114 = f32[128,4,8,128]{0,3,2,1:T(8,128)S(1)} copy(f32[128,4,8,128]{3,0,2,1:T(8,128)} %get-tuple-element.37) | data formatting | bytes 4194304 | tf_op jit(solution)/shard_map/stack | solution.py:72
  86.8 2.2 %fusion.4 = (f32[4096]{0:T(1024)S(1)}, bf16[128,4096]{0,1:T(8,128)(2,1)}) fusion(f32[128,4,8,128]{0,3,2,1:T(8,128)S(1)} %copy.114, bf16[128,4096]{0,1:T(8,128)(2,1)S(1)} %copy-done.1, f32[128,4,8]{0,2,1:T(8,128)S(1)} %get-tuple-element.49, f32[128,32]{0,1:T(8,128)S(1)} %multiply_bitcast_fusion, f32[4096]{0:T(1024)S(1)} %copy-done.35, f32[128,32]{0,1:T(8,128)S(1)} %copy-done.34), kind=kLoop, calls=%fused_computation.8 | loop fusion | flops 5238784 | bytes 4276224 | tf_op jit(solution)/shard_map/reduce_sum | solution.py:24
  89.3 0.8 copy.123
  90.2 0.8 copy.122
  91.0 2.3 %copy.121 = bf16[128,4096]{1,0:T(8,128)(2,1)} copy(bf16[128,4096]{0,1:T(8,128)(2,1)} %get-tuple-element.35) | data formatting | bytes 2097152
  93.3 0.6 dynamic-slice
  94.5 30.9 %all-reduce.5.cloned.1.call-done = bf16[32,1024]{1,0:T(8,128)(2,1)} async-done(((bf16[32,1024]{1,0:T(8,128)(2,1)}), bf16[32,1024]{1,0:T(8,128)(2,1)}) %all-reduce.5.cloned.1.call-update) | async-done | bytes 65552
  125.4 1.4 fusion.123
  127.2 39.3 %all-reduce.2 = (f32[128]{0:T(128)}, f32[128]{0:T(128)}) all-reduce(f32[128]{0:T(128)S(1)} %bitcast_reduce_fusion.1, f32[128]{0:T(128)S(1)} %add.48), channel_id=1, replica_groups=mesh['dp'=4,'group'=8] {'dp','group'}, use_global_device_ids=true, to_apply=%region_17.18 | all-reduce | flops 256 | bytes 2048 | tf_op jit(solution)/shard_map/psum | solution.py:92
  166.5 1.3 fusion.86
  (126 shorter events, 2.7 us)
Async XLA Ops:
  7.2 16.6 %copy-start.14 = (bf16[128,4096]{1,0:T(8,128)(2,1)S(1)}, bf16[128,4096]{1,0:T(8,128)(2,1)}, u32[]{:S(2)}) copy-start(bf16[128,4096]{1,0:T(8,128)(2,1)} %param.9) | copy-start | bytes 3145732
  7.2 118.3 %all-reduce.5.cloned.1.call-start = ((), (), s32[]{:S(2)}) async-start(), calls=%async_computation | async-start | bytes 131072
  8.5 16.2 %copy-start.39 = (f32[512]{0:T(512)}, f32[512]{0:T(512)S(1)}, u32[]{:S(2)}) copy-start(f32[512]{0:T(512)S(1)} %broadcast_bitcast_fusion.3) | copy-start | bytes 6148
  9.2 0.6 copy-start.30
  9.3 0.6 copy-start.41
  9.9 0.6 copy-start.32
  23.5 2.0 %copy-start.37 = (f32[128,4]{0,1:T(4,128)}, f32[128,4]{0,1:T(4,128)S(1)}, u32[]{:S(2)}) copy-start(f32[128,4]{0,1:T(4,128)S(1)} %add_rsqrt_fusion.1) | copy-start | bytes 6148
  24.4 1.6 copy-start
  30.0 3.9 %copy-start.6 = (bf16[128,4,8,128]{3,0,2,1:T(8,128)(2,1)}, bf16[128,4,8,128]{3,0,2,1:T(8,128)(2,1)S(1)}, u32[]{:S(2)}) copy-start(bf16[128,4,8,128]{3,0,2,1:T(8,128)(2,1)S(1)} %multiply_convert_fusion) | copy-start | bytes 3145732
  62.1 3.2 %copy-start.5 = (f32[8,128,160]{1,2,0:T(8,128)S(1)}, f32[8,128,160]{1,2,0:T(8,128)}, u32[]{:S(2)}) copy-start(f32[8,128,160]{1,2,0:T(8,128)} %fusion.50) | copy-start | bytes 1966084
  62.1 4.4 %copy-start.7 = (bf16[128,4,8,128]{3,0,2,1:T(8,128)(2,1)S(1)}, bf16[128,4,8,128]{3,0,2,1:T(8,128)(2,1)}, u32[]{:S(2)}) copy-start(bf16[128,4,8,128]{3,0,2,1:T(8,128)(2,1)} %copy-done.6) | copy-start | bytes 3145732
  62.1 4.6 %copy-start.4 = (f32[8,128,160]{1,2,0:T(8,128)S(1)}, f32[8,128,160]{1,2,0:T(8,128)}, u32[]{:S(2)}) copy-start(f32[8,128,160]{1,2,0:T(8,128)} %fusion.52) | copy-start | bytes 1966084
  63.6 7.2 %copy-start.19 = (bf16[160,1,128]{2,0,1:T(8,128)(2,1)}, bf16[160,1,128]{2,0,1:T(8,128)(2,1)S(1)}, u32[]{:S(2)}) copy-start(bf16[160,1,128]{2,0,1:T(8,128)(2,1)S(1)} %convolution_bitcast_fusion.8) | copy-start | bytes 122884
  63.6 3.4 %copy-start.17 = (bf16[128,1,8,128]{3,0,2,1:T(8,128)(2,1)S(1)}, bf16[128,1,8,128]{3,0,2,1:T(8,128)(2,1)}, u32[]{:S(2)}) copy-start(bf16[128,1,8,128]{3,0,2,1:T(8,128)(2,1)} %copy.137) | copy-start | bytes 786436
  63.6 3.4 %copy-start.29 = (bf16[160,1,128]{2,1,0:T(2,128)(2,1)S(1)}, bf16[160,1,128]{2,1,0:T(2,128)(2,1)}, u32[]{:S(2)}) copy-start(bf16[160,1,128]{2,1,0:T(2,128)(2,1)} %get-tuple-element.43) | copy-start | bytes 122884
  66.5 1.6 copy-start.8
  66.7 1.3 copy-start.3
  67.0 3.7 %copy-start.21 = (bf16[160,1,128]{2,0,1:T(8,128)(2,1)}, bf16[160,1,128]{2,0,1:T(8,128)(2,1)S(1)}, u32[]{:S(2)}) copy-start(bf16[160,1,128]{2,0,1:T(8,128)(2,1)S(1)} %convolution_bitcast_fusion.9) | copy-start | bytes 122884
  67.0 1.4 copy-start.16
  67.0 1.4 copy-start.28
  67.8 1.6 copy-start.9
  68.1 1.3 copy-start.2
  68.3 2.4 %copy-start.23 = (bf16[160,1,128]{2,0,1:T(8,128)(2,1)}, bf16[160,1,128]{2,0,1:T(8,128)(2,1)S(1)}, u32[]{:S(2)}) copy-start(bf16[160,1,128]{2,0,1:T(8,128)(2,1)S(1)} %convolution_bitcast_fusion.10) | copy-start | bytes 122884
  68.3 1.3 copy-start.15
  68.4 1.3 copy-start.27
  69.1 1.6 copy-start.10
  69.7 1.5 copy-start.25
  70.4 0.7 copy-start.12
  70.4 7.1 %copy-start.18 = (bf16[32,4,128]{2,0,1:T(8,128)(2,1)S(1)}, bf16[32,4,128]{2,0,1:T(8,128)(2,1)}, u32[]{:S(2)}) copy-start(bf16[32,4,128]{2,0,1:T(8,128)(2,1)} %copy.94) | copy-start | bytes 98308
  71.1 6.4 %copy-start.11 = (bf16[8,128,160]{1,2,0:T(8,128)(2,1)S(1)}, bf16[8,128,160]{1,2,0:T(8,128)(2,1)}, u32[]{:S(2)}) copy-start(bf16[8,128,160]{1,2,0:T(8,128)(2,1)} %copy-done.10) | copy-start | bytes 983044
  71.2 8.2 %copy-start.13 = (bf16[8,128,160]{1,2,0:T(8,128)(2,1)S(1)}, bf16[8,128,160]{1,2,0:T(8,128)(2,1)}, u32[]{:S(2)}) copy-start(bf16[8,128,160]{1,2,0:T(8,128)(2,1)} %copy-done.12) | copy-start | bytes 983044
  71.8 6.8 %copy-start.20 = (bf16[160,1,128]{2,0,1:T(8,128)(2,1)S(1)}, bf16[160,1,128]{2,0,1:T(8,128)(2,1)}, u32[]{:S(2)}) copy-start(bf16[160,1,128]{2,0,1:T(8,128)(2,1)} %copy-done.19) | copy-start | bytes 122884
  71.9 6.8 %copy-start.22 = (bf16[160,1,128]{2,0,1:T(8,128)(2,1)S(1)}, bf16[160,1,128]{2,0,1:T(8,128)(2,1)}, u32[]{:S(2)}) copy-start(bf16[160,1,128]{2,0,1:T(8,128)(2,1)} %copy-done.21) | copy-start | bytes 122884
  71.9 6.8 %copy-start.24 = (bf16[160,1,128]{2,0,1:T(8,128)(2,1)S(1)}, bf16[160,1,128]{2,0,1:T(8,128)(2,1)}, u32[]{:S(2)}) copy-start(bf16[160,1,128]{2,0,1:T(8,128)(2,1)} %copy-done.23) | copy-start | bytes 122884
  71.9 6.8 %copy-start.26 = (bf16[160,1,128]{2,0,1:T(8,128)(2,1)S(1)}, bf16[160,1,128]{2,0,1:T(8,128)(2,1)}, u32[]{:S(2)}) copy-start(bf16[160,1,128]{2,0,1:T(8,128)(2,1)} %copy-done.25) | copy-start | bytes 122884
  75.3 5.3 %copy-start.38 = (f32[128,4]{0,1:T(4,128)S(1)}, f32[128,4]{0,1:T(4,128)}, u32[]{:S(2)}) copy-start(f32[128,4]{0,1:T(4,128)} %copy-done.37) | copy-start | bytes 6148
  75.3 5.3 %copy-start.43 = (f32[128]{0:T(128)S(1)}, f32[128]{0:T(128)}, u32[]{:S(2)}) copy-start(f32[128]{0:T(128)} %param.16) | copy-start | bytes 1540
  77.5 3.6 %copy-start.45 = (f32[128]{0:T(128)S(1)}, f32[128]{0:T(128)}, u32[]{:S(2)}) copy-start(f32[128]{0:T(128)} %param.15) | copy-start | bytes 1540
  84.7 2.0 %copy-start.1 = (bf16[128,4096]{0,1:T(8,128)(2,1)S(1)}, bf16[128,4096]{0,1:T(8,128)(2,1)}, u32[]{:S(2)}) copy-start(bf16[128,4096]{0,1:T(8,128)(2,1)} %copy-done) | copy-start | bytes 3145732
  84.7 2.1 %copy-start.34 = (f32[128,32]{0,1:T(8,128)S(1)}, f32[128,32]{0,1:T(8,128)}, u32[]{:S(2)}) copy-start(f32[128,32]{0,1:T(8,128)} %get-tuple-element.48) | copy-start | bytes 49156
  84.7 2.1 %copy-start.35 = (f32[4096]{0:T(1024)S(1)}, f32[4096]{0:T(1024)}, u32[]{:S(2)}) copy-start(f32[4096]{0:T(1024)} %broadcast_bitcast_fusion) | copy-start | bytes 49156
  86.8 2.3 %copy-start.42 = (f32[4,4]{1,0:T(4,128)S(1)}, f32[4,4]{1,0:T(4,128)}, u32[]{:S(2)}) copy-start(f32[4,4]{1,0:T(4,128)} %copy-done.41) | copy-start | bytes 196
  86.8 2.4 %copy-start.36 = (bf16[4,512]{1,0:T(4,128)(2,1)S(1)}, bf16[4,512]{1,0:T(4,128)(2,1)}, u32[]{:S(2)}) copy-start(bf16[4,512]{1,0:T(4,128)(2,1)} %param.12) | copy-start | bytes 12292
  86.8 2.3 %slice-start = ((bf16[160,4,128]{2,0,1:T(8,128)(2,1)}), bf16[128,4,128]{2,0,1:T(8,128)(2,1)S(1)}, s32[]{:S(2)}) async-start(bf16[160,4,128]{2,0,1:T(8,128)(2,1)} %maximum_convert_fusion), calls=%async_computation.1 | async-start | bytes 262144 | tf_op jit(solution)/shard_map/slice | solution.py:86
  89.0 4.2 %copy-start.46 = (u32[32]{0:T(128)S(1)}, u32[32]{0:T(128)}, u32[]{:S(2)}) copy-start(u32[32]{0:T(128)} %constant.31) | copy-start | bytes 388
  89.0 37.8 %copy-start.31 = (f32[4,4,128]{2,1,0:T(4,128)S(1)}, f32[4,4,128]{2,1,0:T(4,128)}, u32[]{:S(2)}) copy-start(f32[4,4,128]{2,1,0:T(4,128)} %copy-done.30) | copy-start | bytes 24580
  89.0 37.8 %copy-start.44 = (f32[128]{0:T(128)S(1)}, f32[128]{0:T(128)}, u32[]{:S(2)}) copy-start(f32[128]{0:T(128)} %param.16) | copy-start | bytes 1540
  89.0 77.5 %copy-start.33 = (f32[1,4,4,128]{3,2,1,0:T(4,128)S(1)}, f32[1,4,4,128]{3,2,1,0:T(4,128)}, u32[]{:S(2)}) copy-start(f32[1,4,4,128]{3,2,1,0:T(4,128)} %copy-done.32) | copy-start | bytes 24580
  89.0 77.5 %copy-start.40 = (f32[512]{0:T(512)S(1)}, f32[512]{0:T(512)}, u32[]{:S(2)}) copy-start(f32[512]{0:T(512)} %copy-done.39) | copy-start | bytes 6148
Sparse Core Ops, SparseCore 0:
  72.0 53.4 all-reduce.4
where the time goes:
time: 176 us; the launch traced here: 175 us
  blocking collectives  59.1 us (34%)
  waiting for transfers between devices  31 us (18%)
  local copies, waits for them, and re-layouts  27.1 us (15%)
  matrix products  22.8 us (13%)
  other arithmetic  18.5 us (11%)
  between operations  16.1 us (9%)
    psum x1, blocking collectives, local(): lax.psum((gain_query, gain_comp + gain_prompt), ('dp', 'group'))  39.3 us
    unnamed x2, waiting for transfers between devices  31 us
    unnamed x108, local copies, waits for them, and re-layouts  17.3 us
    all_gather x1, blocking collectives, local(): lax.all_gather(pnorm.reshape(shard, HK * HD), 'group', axis=0, tiled=True)  10.6 us
    all_gather x1, blocking collectives, local(): lax.all_gather(prompt_value, 'group', axis=0, tiled=True)  9.25 us
    div x4, matrix products, head_grads(): dscore = (expo / totals * (dprob - delta)).astype(jnp.bfloat16)  8.01 us
    dot_general x4, matrix products, head_grads(): jnp.einsum('gck,kd->cgd', dscore, key_head, preferred_element_type=jnp.fl...  6.62 us
    reduce_sum x2, other arithmetic, norm_back(): jnp.mean(scaled * unit, axis=-1, keepdims=True)  3.73 us
  transfers between devices with their start and end apart: 1, of which 1 were waited for; matrix products, arithmetic and copies ran while one was open for 12% of the time, Pallas kernels for 0%

commit v1 on v0

v1 whole, which is shorter than its diff:
```python
import functools
import math

import jax
import jax.numpy as jnp
from jax import lax
from jax.experimental import pallas as pl
from jax.experimental.pallas import tpu as pltpu
from jax.sharding import PartitionSpec as P

HD = 128
HQ = 32
HK = 4
GROUPS = HQ // HK
EPS = 1e-06
SCALE = HD ** (-0.5)
LOG2E = math.log2(math.e)
MESH = pl.DeviceIdType.MESH
F32 = jnp.float32
BF16 = jnp.bfloat16


def dot_nt(a, b):
    return lax.dot_general(a, b, (((1,), (1,)), ((), ())), preferred_element_type=F32)


def dot_tn(a, b):
    return lax.dot_general(a, b, (((0,), (0,)), ((), ())), preferred_element_type=F32)


def kernel(
    n, nd,
    len_ref, q_hbm, ck_hbm, cv_hbm, pk_hbm, pv_hbm, do_hbm, qg_ref, kg_ref,
    dq_hbm, dck_hbm, dcv_hbm, dpk_hbm, dpv_hbm, gq_ref, gk_ref,
    qv, dov, ckv, vv, pkb, pvb, pf, pvf, uu, kgs, ss, dd, ee, rss, tots, dss, cs, ws, dvs,
    stg, share, rbuf, gbuf, hbuf, dqv, dckv, dcvv, dpkv, dpvv,
    q_sem, do_sem, in_sem, out_sem, dq_sem, pks, pkr, pvs, pvr, shs, shr, gs, gr, hs, hr,
):
    dp = lax.axis_index("dp")
    me = lax.axis_index("group")
    count = q_hbm.shape[0]
    shard = pk_hbm.shape[0]
    plen = shard * n
    width = GROUPS * HD
    total = plen + count

    def peer(k):
        return (dp, lax.rem(me + k, n))

    def dpeer(k):
        return (lax.rem(dp + k, nd), me)

    barrier = pltpu.get_barrier_semaphore()
    for k in range(1, n):
        pl.semaphore_signal(barrier, inc=1, device_id=peer(k), device_id_type=MESH)
    for k in range(1, nd):
        pl.semaphore_signal(barrier, inc=1, device_id=dpeer(k), device_id_type=MESH)

    ins = [
        pltpu.make_async_copy(ck_hbm, ckv, in_sem.at[0]),
        pltpu.make_async_copy(cv_hbm, vv.at[pl.ds(plen, count)], in_sem.at[1]),
        pltpu.make_async_copy(pk_hbm, pkb.at[0], in_sem.at[2]),
        pltpu.make_async_copy(pv_hbm, pvb.at[0], in_sem.at[3]),
    ]
    for c in ins:
        c.start()
    q_in, do_in = [], []
    for g in range(HK):
        cols = pl.ds(g * width, width)
        q_in.append(pltpu.make_async_copy(q_hbm.at[:, cols], qv.at[:, cols], q_sem.at[g]))
        do_in.append(pltpu.make_async_copy(do_hbm.at[:, cols], dov.at[:, cols], do_sem.at[g]))
        q_in[g].start()
        do_in[g].start()

    pl.semaphore_wait(barrier, n - 1 + nd - 1)
    gathers = []
    for k in range(1, n):
        for src, buf, ssem, rsem in ((pk_hbm, pkb, pks, pkr), (pv_hbm, pvb, pvs, pvr)):
            c = pltpu.make_async_remote_copy(
                src_ref=src, dst_ref=buf.at[k], send_sem=ssem.at[k - 1], recv_sem=rsem.at[k - 1],
                device_id=peer(k), device_id_type=MESH)
            c.start()
            gathers.append(c)

    gain = qg_ref[...] * kg_ref[...]

    def key_norm(x):
        return lax.rsqrt(jnp.mean(x * x, axis=-1, keepdims=True) + EPS)

    ins[0].wait()
    ins[1].wait()
    for h in range(HK):
        hc = slice(h * HD, (h + 1) * HD)
        x = ckv[:, hc].astype(F32)
        u = x * key_norm(x)
        uu[plen:total, hc] = u
        kgs[plen:total, hc] = (u * gain).astype(BF16)

    krow = lax.broadcasted_iota(jnp.int32, (count, 2 * HD), 0)
    qcol = lax.broadcasted_iota(jnp.int32, (count, 2 * HD), 1)
    seen = krow <= jnp.where(qcol >= HD, qcol - HD, qcol)
    live = qcol[0:1]
    live = jnp.where(live >= HD, live - HD, live) < len_ref[0]
    ones = jnp.ones((8, HD), BF16)

    def pair(ref, c0):
        return jnp.concatenate([ref[:, c0:c0 + HD], ref[:, c0 + HD:c0 + 2 * HD]], axis=0)

    for g in range(HK):
        hc = slice(g * HD, (g + 1) * HD)
        q_in[g].wait()
        do_in[g].wait()
        for j in range(GROUPS // 2):
            c0 = g * width + j * 2 * HD
            cc = slice(c0, c0 + 2 * HD)
            x = pair(qv, c0)
            go = pair(dov, c0)
            ms = dot_nt(ones, x * x)[0:1]
            r = lax.rsqrt(ms * (1.0 / HD) + EPS)
            rs = r * SCALE
            s = dot_nt(kgs[plen:total, hc], x)
            d = dot_nt(vv[plen:total, hc], go)
            e = jnp.where(seen, jnp.exp2(s * (rs * LOG2E)), 0.0)
            ss[:, cc] = s
            dd[:, cc] = d
            ee[:, cc] = e
            rss[0:1, cc] = r
            tots[0:1, cc] = jnp.sum(e, axis=0, keepdims=True)
            tots[1:2, cc] = jnp.sum(e * d, axis=0, keepdims=True)

    ins[2].wait()
    ins[3].wait()
    for c in gathers:
        c.wait_recv()
    for k in range(n):
        pf[k * shard:(k + 1) * shard, :] = pkb[k].astype(F32)
        pvf[k * shard:(k + 1) * shard, :] = pvb[k].astype(F32)
    for h in range(HK):
        hc = slice(h * HD, (h + 1) * HD)
        x = pf[:, hc]
        u = x * key_norm(x)
        uu[0:plen, hc] = u
        kgs[0:plen, hc] = (u * gain).astype(BF16)
    vv[0:plen, :] = pvf[...].astype(BF16)

    tsum = jnp.zeros((1, HD), F32)
    for g in range(HK):
        hc = slice(g * HD, (g + 1) * HD)
        w = jnp.zeros((total, HD), F32)
        dv = jnp.zeros((total, HD), F32)
        for j in range(GROUPS // 2):
            c0 = g * width + j * 2 * HD
            cc = slice(c0, c0 + 2 * HD)
            x = pair(qv, c0)
            go = pair(dov, c0)
            r = rss[0:1, cc]
            rs = r * SCALE
            sp = dot_nt(kgs[0:plen, hc], x)
            dpr = dot_nt(vv[0:plen, hc], go)
            ep = jnp.exp2(sp * (rs * LOG2E))
            tot = tots[0:1, cc] + jnp.sum(ep, axis=0, keepdims=True)
            t2 = tots[1:2, cc] + jnp.sum(ep * dpr, axis=0, keepdims=True)
            inv = 1.0 / tot
            delta = t2 * inv
            inv = jnp.where(live, inv, 0.0)
            pp = ep * inv
            dsp = pp * ((dpr - delta) * rs)
            pc = ee[:, cc] * inv
            dsc = pc * ((dd[:, cc] - delta) * rs)
            m = (jnp.sum(dsp * sp, axis=0, keepdims=True)
                 + jnp.sum(dsc * ss[:, cc], axis=0, keepdims=True))
            c = r * r * m * (1.0 / HD)
            hh = g * GROUPS + 2 * j
            cs[hh:hh + 1, :] = c[:, 0:HD]
            cs[hh + 1:hh + 2, :] = c[:, HD:2 * HD]
            pw = jnp.concatenate([pp.astype(BF16), pc.astype(BF16)], axis=0)
            ds = jnp.concatenate([dsp.astype(BF16), dsc.astype(BF16)], axis=0)
            dss[:, cc] = ds
            w = w + jnp.dot(ds, x, preferred_element_type=F32)
            dv = dv + jnp.dot(pw, go, preferred_element_type=F32)
        ws[:, hc] = w
        dvs[:, hc] = dv
        tsum = tsum + jnp.sum(w * uu[:, hc], axis=0, keepdims=True)

    gbuf[me] = tsum
    for k in range(n):
        stg[k, 0:shard, :] = ws[k * shard:(k + 1) * shard, :]
        stg[k, shard:2 * shard, :] = dvs[k * shard:(k + 1) * shard, :]
        if k:
            share[k] = stg[k].astype(BF16)
    gains, shares = [], []
    for k in range(1, n):
        c = pltpu.make_async_remote_copy(
            src_ref=gbuf.at[me], dst_ref=gbuf.at[me], send_sem=gs.at[k - 1], recv_sem=gr.at[k - 1],
            device_id=peer(k), device_id_type=MESH)
        c.start()
        gains.append(c)
    for k in range(1, n):
        c = pltpu.make_async_remote_copy(
            src_ref=share.at[k], dst_ref=rbuf.at[k - 1], send_sem=shs.at[k - 1],
            recv_sem=shr.at[k - 1], device_id=peer(n - k), device_id_type=MESH)
        c.start()
        shares.append(c)

    ct = jnp.transpose(cs[...])
    outs = []

    def dq_group(g):
        hc = slice(g * HD, (g + 1) * HD)
        for j in range(GROUPS // 2):
            c0 = g * width + j * 2 * HD
            a = dot_tn(dss[:, c0:c0 + 2 * HD], kgs[:, hc])
            hh = g * GROUPS + 2 * j
            for i in range(2):
                col = slice(c0 + i * HD, c0 + (i + 1) * HD)
                x = qv[:, col].astype(F32)
                dqv[:, col] = (a[i * HD:(i + 1) * HD] - x * ct[:, hh + i:hh + i + 1]).astype(BF16)
        cols = pl.ds(g * width, width)
        c = pltpu.make_async_copy(dqv.at[:, cols], dq_hbm.at[:, cols], dq_sem.at[g])
        c.start()
        outs.append(c)

    for g in range(HK):
        dq_group(g)

    def back(w, u, x):
        a = w * gain
        return key_norm(x) * (a - u * jnp.mean(a * u, axis=-1, keepdims=True))

    for h in range(HK):
        hc = slice(h * HD, (h + 1) * HD)
        x = ckv[:, hc].astype(F32)
        dckv[:, hc] = back(ws[plen:total, hc], uu[plen:total, hc], x).astype(BF16)
    dcvv[...] = dvs[plen:total, :].astype(BF16)
    for i, (src, dst) in enumerate(((dckv, dck_hbm), (dcvv, dcv_hbm))):
        c = pltpu.make_async_copy(src, dst, out_sem.at[i])
        c.start()
        outs.append(c)

    for c in gains:
        c.wait_recv()
    tg = gbuf[0]
    for k in range(1, n):
        tg = tg + gbuf[k]
    hbuf[dp] = tg
    dgains = []
    for k in range(1, nd):
        c = pltpu.make_async_remote_copy(
            src_ref=hbuf.at[dp], dst_ref=hbuf.at[dp], send_sem=hs.at[k - 1], recv_sem=hr.at[k - 1],
            device_id=dpeer(k), device_id_type=MESH)
        c.start()
        dgains.append(c)

    for c in shares:
        c.wait_recv()
    acc = stg[0]
    for k in range(n - 1):
        acc = acc + rbuf[k].astype(F32)
    for h in range(HK):
        hc = slice(h * HD, (h + 1) * HD)
        dx = back(acc[0:shard, hc], uu[0:shard, hc], pf[0:shard, hc])
        dpkv[:, hc] = dx.astype(BF16)
    dpvv[...] = acc[shard:2 * shard].astype(BF16)
    for i, (src, dst) in enumerate(((dpkv, dpk_hbm), (dpvv, dpv_hbm))):
        c = pltpu.make_async_copy(src, dst, out_sem.at[2 + i])
        c.start()
        outs.append(c)

    for c in dgains:
        c.wait_recv()
    tt = hbuf[0]
    for k in range(1, nd):
        tt = tt + hbuf[k]
    gq_ref[...] = tt * kg_ref[...]
    gk_ref[...] = tt * qg_ref[...]
    for c in outs:
        c.wait()
    for c in gathers + gains + shares + dgains:
        c.wait_send()


def local(n, nd, query, comp_key, comp_value, prompt_key, prompt_value, d_out, q_gain, k_gain, lengths):
    count = query.shape[0]
    shard = prompt_key.shape[0]
    plen = shard * n
    total = plen + count
    wq, wk = HQ * HD, HK * HD
    any_spec = pl.BlockSpec(memory_space=pl.ANY)
    vmem = pl.BlockSpec(memory_space=pltpu.VMEM)
    dma = pltpu.SemaphoreType.DMA
    np_, nd_ = max(n - 1, 1), max(nd - 1, 1)
    res = pl.pallas_call(
        functools.partial(kernel, n, nd),
        out_shape=(
            jax.ShapeDtypeStruct((count, wq), BF16),
            jax.ShapeDtypeStruct((count, wk), BF16),
            jax.ShapeDtypeStruct((count, wk), BF16),
            jax.ShapeDtypeStruct((shard, wk), BF16),
            jax.ShapeDtypeStruct((shard, wk), BF16),
            jax.ShapeDtypeStruct((1, HD), F32),
            jax.ShapeDtypeStruct((1, HD), F32),
        ),
        in_specs=[pl.BlockSpec(memory_space=pltpu.SMEM)] + [any_spec] * 6 + [vmem] * 2,
        out_specs=[any_spec] * 5 + [vmem] * 2,
        scratch_shapes=[
            pltpu.VMEM((count, wq), BF16),
            pltpu.VMEM((count, wq), BF16),
            pltpu.VMEM((count, wk), BF16),
            pltpu.VMEM((total, wk), BF16),
            pltpu.VMEM((n, shard, wk), BF16),
            pltpu.VMEM((n, shard, wk), BF16),
            pltpu.VMEM((plen, wk), F32),
            pltpu.VMEM((plen, wk), F32),
            pltpu.VMEM((total, wk), F32),
            pltpu.VMEM((total, wk), BF16),
            pltpu.VMEM((count, wq), F32),
            pltpu.VMEM((count, wq), F32),
            pltpu.VMEM((count, wq), F32),
            pltpu.VMEM((8, wq), F32),
            pltpu.VMEM((8, wq), F32),
            pltpu.VMEM((total, wq), BF16),
            pltpu.VMEM((HQ, HD), F32),
            pltpu.VMEM((total, wk), F32),
            pltpu.VMEM((total, wk), F32),
            pltpu.VMEM((n, 2 * shard, wk), F32),
            pltpu.VMEM((n, 2 * shard, wk), BF16),
            pltpu.VMEM((np_, 2 * shard, wk), BF16),
            pltpu.VMEM((n, 1, HD), F32),
            pltpu.VMEM((nd, 1, HD), F32),
            pltpu.VMEM((count, wq), BF16),
            pltpu.VMEM((count, wk), BF16),
            pltpu.VMEM((count, wk), BF16),
            pltpu.VMEM((shard, wk), BF16),
            pltpu.VMEM((shard, wk), BF16),
            dma((HK,)), dma((HK,)), dma((4,)), dma((4,)), dma((HK,)),
            dma((np_,)), dma((np_,)), dma((np_,)), dma((np_,)),
            dma((np_,)), dma((np_,)), dma((np_,)), dma((np_,)),
            dma((nd_,)), dma((nd_,)),
        ],
        compiler_params=pltpu.CompilerParams(
            collective_id=0, has_side_effects=True, vmem_limit_bytes=48 * 1024 * 1024),
        name="gqa_back",
    )(lengths, query, comp_key, comp_value, prompt_key, prompt_value, d_out,
      q_gain.reshape(1, HD), k_gain.reshape(1, HD))
    return (*res[:5], res[5].reshape(HD), res[6].reshape(HD))


def solution(mesh):
    n, nd = mesh.shape["group"], mesh.shape["dp"]
    row = P(("dp", "group"), None)
    return jax.shard_map(
        functools.partial(local, n, nd),
        mesh=mesh,
        in_specs=(row, row, row, row, row, row, P(), P(), P(("dp", "group"))),
        out_specs=(row, row, row, row, row, P(), P()),
        check_vma=False,
    )
```

time: 176 us -> 31 us (0.18)
  blocking collectives: 59.1 us -> 0 us
  waiting for transfers between devices: 31 us -> 0 us
  matrix products: 22.8 us -> 0 us
  Pallas kernels: 0 us -> 19.3 us
  other arithmetic: 18.5 us -> 0 us
  local copies, waits for them, and re-layouts: 27.1 us -> 10.1 us
  between operations: 16.1 us -> 1.34 us
    psum x1 -> x0, blocking collectives: 39.3 us -> none  [local(): lax.psum((gain_query, gain_comp + gain_prompt), ('dp', 'group'))]
    unnamed x2 -> x0, waiting for transfers between devices: 31 us -> none
    all_gather x2 -> x0, blocking collectives: 19.8 us -> none  [the longest x1 10.6 us: local(): lax.all_gather(pnorm.reshape(shard, HK * HD), 'group', axis=0, tiled=True)]
    pallas_call x0 -> x1, Pallas kernels: none -> 19.3 us  [local(): pl.pallas_call(functools.partial(kernel, n, nd), out_shape=(jax.ShapeDtyp...]
    dot_general x20 -> x0, matrix products: 14.8 us -> none  [the longest x4 6.62 us: head_grads(): jnp.einsum('gck,kd->cgd', dscore, key_head, preferred_element_type=jnp.fl...]
    div x4 -> x0, matrix products: 8.01 us -> none  [head_grads(): dscore = (expo / totals * (dprob - delta)).astype(jnp.bfloat16)]
    unnamed x108 -> x23, local copies, waits for them, and re-layouts: 17.3 us -> 10.1 us
    reduce_sum x9 -> x0, other arithmetic: 6.64 us -> none  [the longest x2 3.73 us: norm_back(): jnp.mean(scaled * unit, axis=-1, keepdims=True)]
  transfers between devices with their start and end apart: 1 -> 0, of which waited for: 1 -> 0; matrix products, arithmetic and copies ran while one was open for 12% -> 0% of each run, Pallas kernels for 0% -> 0%
where the time goes in v1:
time: 31 us; the launch traced here: 30.7 us
  Pallas kernels  19.3 us (62%)
  local copies, waits for them, and re-layouts  10.1 us (33%)
  between operations  1.34 us (4%)
    pallas_call x1, Pallas kernels, local(): pl.pallas_call(functools.partial(kernel, n, nd), out_shape=(jax.ShapeDtyp...  19.3 us
    unnamed x23, local copies, waits for them, and re-layouts  10.1 us

profile of v1, /device:TPU:0, one launch (start us, length us, event | category | flops | bytes accessed | tf_op | source)
XLA Modules:
  0.0 30.7 jit_solution(4439993326060228996)
XLA Ops:
  0.6 0.0 copy-start.4
  1.3 0.0 copy-start.6
  1.3 0.0 copy-start.7
  1.3 0.0 copy-done.4
  1.3 0.6 %copy-done.6 = f32[128]{0:T(128)S(1)} copy-done((f32[128]{0:T(128)S(1)}, f32[128]{0:T(128)}, u32[]{:S(2)}) %copy-start.6) | copy-done | bytes 536
  2.0 0.0 copy-done.7
  2.0 0.0 copy-start
  2.0 1.2 %copy-done = bf16[128,4096]{1,0:T(8,128)(2,1)S(1)} copy-done((bf16[128,4096]{1,0:T(8,128)(2,1)S(1)}, bf16[128,4096]{1,0:T(8,128)(2,1)}, u32[]{:S(2)}) %copy-start) | copy-done | bytes 1048600
  3.2 0.0 copy-start.1
  3.2 1.2 %copy-done.1 = bf16[128,4096]{1,0:T(8,128)(2,1)S(1)} copy-done((bf16[128,4096]{1,0:T(8,128)(2,1)S(1)}, bf16[128,4096]{1,0:T(8,128)(2,1)}, u32[]{:S(2)}) %copy-start.1) | copy-done | bytes 1048600
  4.4 0.0 copy-start.2
  4.4 0.9 %copy-done.2 = bf16[128,512]{1,0:T(8,128)(2,1)S(1)} copy-done((bf16[128,512]{1,0:T(8,128)(2,1)S(1)}, bf16[128,512]{1,0:T(8,128)(2,1)}, u32[]{:S(2)}) %copy-start.2) | copy-done | bytes 131096
  5.3 0.0 copy-start.3
  5.3 0.9 %copy-done.3 = bf16[128,512]{1,0:T(8,128)(2,1)S(1)} copy-done((bf16[128,512]{1,0:T(8,128)(2,1)S(1)}, bf16[128,512]{1,0:T(8,128)(2,1)}, u32[]{:S(2)}) %copy-start.3) | copy-done | bytes 131096
  6.2 0.0 copy-start.5
  6.2 0.7 %copy-done.5 = bf16[4,512]{1,0:T(4,128)(2,1)S(1)} copy-done((bf16[4,512]{1,0:T(4,128)(2,1)S(1)}, bf16[4,512]{1,0:T(4,128)(2,1)}, u32[]{:S(2)}) %copy-start.5) | copy-done | bytes 4120
  6.9 19.3 %gqa_back.1 = (bf16[128,4096]{1,0:T(8,128)(2,1)S(1)}, bf16[128,512]{1,0:T(8,128)(2,1)S(1)}, bf16[128,512]{1,0:T(8,128)(2,1)S(1)}, bf16[4,512]{1,0:T(4,128)(2,1)S...) custom-call(s32[1]{0:T(128)S(6)} %copy.23.len_ref, bf16[128,4096]{1,0:T(8,128)(2,1)S(1)} %copy-done, ...), custom_call_target="tpu_custom_call" | custom-call | tf_op jit(solution)/shard_map/gqa_back/pallas_call | solution.py:292
  26.2 1.0 %copy.24 = bf16[128,4096]{1,0:T(8,128)(2,1)} copy(bf16[128,4096]{1,0:T(8,128)(2,1)S(1)} %get-tuple-element.28) | data formatting | bytes 2097152
  27.2 0.7 %copy.25 = bf16[128,512]{1,0:T(8,128)(2,1)} copy(bf16[128,512]{1,0:T(8,128)(2,1)S(1)} %get-tuple-element.29) | data formatting | bytes 262144
  27.8 0.7 %copy.26 = bf16[128,512]{1,0:T(8,128)(2,1)} copy(bf16[128,512]{1,0:T(8,128)(2,1)S(1)} %get-tuple-element.30) | data formatting | bytes 262144
  28.5 0.6 %copy.27 = bf16[4,512]{1,0:T(4,128)(2,1)} copy(bf16[4,512]{1,0:T(4,128)(2,1)S(1)} %get-tuple-element.31) | data formatting | bytes 8192
  29.1 0.6 %copy.28 = bf16[4,512]{1,0:T(4,128)(2,1)} copy(bf16[4,512]{1,0:T(4,128)(2,1)S(1)} %get-tuple-element.32) | data formatting | bytes 8192
  29.7 0.5 %copy.29 = f32[128]{0:T(128)} copy(f32[128]{0:T(128)S(1)} %bitcast.7) | data formatting | bytes 1024
  30.2 0.5 %copy.30 = f32[128]{0:T(128)} copy(f32[128]{0:T(128)S(1)} %bitcast.6) | data formatting | bytes 1024
Async XLA Ops:
  0.6 0.7 %copy-start.4 = (bf16[4,512]{1,0:T(4,128)(2,1)S(1)}, bf16[4,512]{1,0:T(4,128)(2,1)}, u32[]{:S(2)}) copy-start(bf16[4,512]{1,0:T(4,128)(2,1)} %pk_hbm.1) | copy-start | bytes 12292
  1.3 0.7 %copy-start.6 = (f32[128]{0:T(128)S(1)}, f32[128]{0:T(128)}, u32[]{:S(2)}) copy-start(f32[128]{0:T(128)} %param.15) | copy-start | bytes 1540
  1.3 0.7 %copy-start.7 = (f32[128]{0:T(128)S(1)}, f32[128]{0:T(128)}, u32[]{:S(2)}) copy-start(f32[128]{0:T(128)} %param.16) | copy-start | bytes 1540
  2.0 1.2 %copy-start = (bf16[128,4096]{1,0:T(8,128)(2,1)S(1)}, bf16[128,4096]{1,0:T(8,128)(2,1)}, u32[]{:S(2)}) copy-start(bf16[128,4096]{1,0:T(8,128)(2,1)} %q_hbm.1) | copy-start | bytes 3145732
  3.2 1.2 %copy-start.1 = (bf16[128,4096]{1,0:T(8,128)(2,1)S(1)}, bf16[128,4096]{1,0:T(8,128)(2,1)}, u32[]{:S(2)}) copy-start(bf16[128,4096]{1,0:T(8,128)(2,1)} %do_hbm.1) | copy-start | bytes 3145732
  4.4 0.9 %copy-start.2 = (bf16[128,512]{1,0:T(8,128)(2,1)S(1)}, bf16[128,512]{1,0:T(8,128)(2,1)}, u32[]{:S(2)}) copy-start(bf16[128,512]{1,0:T(8,128)(2,1)} %ck_hbm.1) | copy-start | bytes 393220
  5.3 0.9 %copy-start.3 = (bf16[128,512]{1,0:T(8,128)(2,1)S(1)}, bf16[128,512]{1,0:T(8,128)(2,1)}, u32[]{:S(2)}) copy-start(bf16[128,512]{1,0:T(8,128)(2,1)} %cv_hbm.1) | copy-start | bytes 393220
  6.2 0.7 %copy-start.5 = (bf16[4,512]{1,0:T(4,128)(2,1)S(1)}, bf16[4,512]{1,0:T(4,128)(2,1)}, u32[]{:S(2)}) copy-start(bf16[4,512]{1,0:T(4,128)(2,1)} %pv_hbm.1) | copy-start | bytes 12292

commit v2 on v1

--- a/solution.py
+++ b/solution.py
@@ -30,11 +30,12 @@
 
 def kernel(
     n, nd,
-    len_ref, q_hbm, ck_hbm, cv_hbm, pk_hbm, pv_hbm, do_hbm, qg_ref, kg_ref,
-    dq_hbm, dck_hbm, dcv_hbm, dpk_hbm, dpv_hbm, gq_ref, gk_ref,
+    len_hbm, q_hbm, ck_hbm, cv_hbm, pk_hbm, pv_hbm, do_hbm, qg_hbm, kg_hbm,
+    dqv, dckv, dcvv, dpkv, dpvv, gq_ref, gk_ref,
+    len_ref, qg_ref, kg_ref,
     qv, dov, ckv, vv, pkb, pvb, pf, pvf, uu, kgs, ss, dd, ee, rss, tots, dss, cs, ws, dvs,
-    stg, share, rbuf, gbuf, hbuf, dqv, dckv, dcvv, dpkv, dpvv,
-    q_sem, do_sem, in_sem, out_sem, dq_sem, pks, pkr, pvs, pvr, shs, shr, gs, gr, hs, hr,
+    stg, share, rbuf, gbuf, hbuf,
+    q_sem, do_sem, in_sem, pks, pkr, pvs, pvr, shs, shr, gs, gr, hs, hr,
 ):
     dp = lax.axis_index("dp")
     me = lax.axis_index("group")
@@ -61,6 +62,9 @@
         pltpu.make_async_copy(cv_hbm, vv.at[pl.ds(plen, count)], in_sem.at[1]),
         pltpu.make_async_copy(pk_hbm, pkb.at[0], in_sem.at[2]),
         pltpu.make_async_copy(pv_hbm, pvb.at[0], in_sem.at[3]),
+        pltpu.make_async_copy(qg_hbm, qg_ref, in_sem.at[4]),
+        pltpu.make_async_copy(kg_hbm, kg_ref, in_sem.at[5]),
+        pltpu.make_async_copy(len_hbm, len_ref, in_sem.at[6]),
     ]
     for c in ins:
         c.start()
@@ -82,6 +86,8 @@
             c.start()
             gathers.append(c)
 
+    for c in ins[4:]:
+        c.wait()
     gain = qg_ref[...] * kg_ref[...]
 
     def key_norm(x):
@@ -203,7 +209,6 @@
         shares.append(c)
 
     ct = jnp.transpose(cs[...])
-    outs = []
 
     def dq_group(g):
         hc = slice(g * HD, (g + 1) * HD)
@@ -215,10 +220,6 @@
                 col = slice(c0 + i * HD, c0 + (i + 1) * HD)
                 x = qv[:, col].astype(F32)
                 dqv[:, col] = (a[i * HD:(i + 1) * HD] - x * ct[:, hh + i:hh + i + 1]).astype(BF16)
-        cols = pl.ds(g * width, width)
-        c = pltpu.make_async_copy(dqv.at[:, cols], dq_hbm.at[:, cols], dq_sem.at[g])
-        c.start()
-        outs.append(c)
 
     for g in range(HK):
         dq_group(g)
@@ -232,10 +233,6 @@
         x = ckv[:, hc].astype(F32)
         dckv[:, hc] = back(ws[plen:total, hc], uu[plen:total, hc], x).astype(BF16)
     dcvv[...] = dvs[plen:total, :].astype(BF16)
-    for i, (src, dst) in enumerate(((dckv, dck_hbm), (dcvv, dcv_hbm))):
-        c = pltpu.make_async_copy(src, dst, out_sem.at[i])
-        c.start()
-        outs.append(c)
 
     for c in gains:
         c.wait_recv()
@@ -261,10 +258,6 @@
         dx = back(acc[0:shard, hc], uu[0:shard, hc], pf[0:shard, hc])
         dpkv[:, hc] = dx.astype(BF16)
     dpvv[...] = acc[shard:2 * shard].astype(BF16)
-    for i, (src, dst) in enumerate(((dpkv, dpk_hbm), (dpvv, dpv_hbm))):
-        c = pltpu.make_async_copy(src, dst, out_sem.at[2 + i])
-        c.start()
-        outs.append(c)
 
     for c in dgains:
         c.wait_recv()
@@ -273,10 +266,17 @@
         tt = tt + hbuf[k]
     gq_ref[...] = tt * kg_ref[...]
     gk_ref[...] = tt * qg_ref[...]
-    for c in outs:
-        c.wait()
     for c in gathers + gains + shares + dgains:
         c.wait_send()
+
+
+def put_out(*refs):
+    sem = refs[14]
+    copies = [pltpu.make_async_copy(refs[i], refs[7 + i], sem.at[i]) for i in range(7)]
+    for c in copies:
+        c.start()
+    for c in copies:
+        c.wait()
 
 
 def local(n, nd, query, comp_key, comp_value, prompt_key, prompt_value, d_out, q_gain, k_gain, lengths):
@@ -285,24 +285,28 @@
     plen = shard * n
     total = plen + count
     wq, wk = HQ * HD, HK * HD
-    any_spec = pl.BlockSpec(memory_space=pl.ANY)
+    hbm = pl.BlockSpec(memory_space=pltpu.HBM)
     vmem = pl.BlockSpec(memory_space=pltpu.VMEM)
     dma = pltpu.SemaphoreType.DMA
     np_, nd_ = max(n - 1, 1), max(nd - 1, 1)
+    shapes = (
+        jax.ShapeDtypeStruct((count, wq), BF16),
+        jax.ShapeDtypeStruct((count, wk), BF16),
+        jax.ShapeDtypeStruct((count, wk), BF16),
+        jax.ShapeDtypeStruct((shard, wk), BF16),
+        jax.ShapeDtypeStruct((shard, wk), BF16),
+        jax.ShapeDtypeStruct((1, HD), F32),
+        jax.ShapeDtypeStruct((1, HD), F32),
+    )
     res = pl.pallas_call(
         functools.partial(kernel, n, nd),
-        out_shape=(
-            jax.ShapeDtypeStruct((count, wq), BF16),
-            jax.ShapeDtypeStruct((count, wk), BF16),
-            jax.ShapeDtypeStruct((count, wk), BF16),
-            jax.ShapeDtypeStruct((shard, wk), BF16),
-            jax.ShapeDtypeStruct((shard, wk), BF16),
-            jax.ShapeDtypeStruct((1, HD), F32),
-            jax.ShapeDtypeStruct((1, HD), F32),
-        ),
-        in_specs=[pl.BlockSpec(memory_space=pltpu.SMEM)] + [any_spec] * 6 + [vmem] * 2,
-        out_specs=[any_spec] * 5 + [vmem] * 2,
+        out_shape=shapes,
+        in_specs=[hbm] * 9,
+        out_specs=[vmem] * 7,
         scratch_shapes=[
+            pltpu.SMEM((1,), jnp.int32),
+            pltpu.VMEM((1, HD), F32),
+            pltpu.VMEM((1, HD), F32),
             pltpu.VMEM((count, wq), BF16),
             pltpu.VMEM((count, wq), BF16),
             pltpu.VMEM((count, wk), BF16),
@@ -327,12 +331,7 @@
             pltpu.VMEM((np_, 2 * shard, wk), BF16),
             pltpu.VMEM((n, 1, HD), F32),
             pltpu.VMEM((nd, 1, HD), F32),
-            pltpu.VMEM((count, wq), BF16),
-            pltpu.VMEM((count, wk), BF16),
-            pltpu.VMEM((count, wk), BF16),
-            pltpu.VMEM((shard, wk), BF16),
-            pltpu.VMEM((shard, wk), BF16),
-            dma((HK,)), dma((HK,)), dma((4,)), dma((4,)), dma((HK,)),
+            dma((HK,)), dma((HK,)), dma((7,)),
             dma((np_,)), dma((np_,)), dma((np_,)), dma((np_,)),
             dma((np_,)), dma((np_,)), dma((np_,)), dma((np_,)),
             dma((nd_,)), dma((nd_,)),
@@ -342,6 +341,15 @@
         name="gqa_back",
     )(lengths, query, comp_key, comp_value, prompt_key, prompt_value, d_out,
       q_gain.reshape(1, HD), k_gain.reshape(1, HD))
+    res = pl.pallas_call(
+        put_out,
+        out_shape=shapes,
+        in_specs=[pl.BlockSpec(memory_space=pl.ANY)] * 7,
+        out_specs=[hbm] * 7,
+        scratch_shapes=[dma((7,))],
+        compiler_params=pltpu.CompilerParams(vmem_limit_bytes=1024 * 1024),
+        name="put_out",
+    )(*res)
     return (*res[:5], res[5].reshape(HD), res[6].reshape(HD))
 
 

time: 31 us -> 27.7 us (0.89)
  local copies, waits for them, and re-layouts: 10.1 us -> 5.59 us
  Pallas kernels: 19.3 us -> 20.4 us
    unnamed x23 -> x16, local copies, waits for them, and re-layouts: 10.1 us -> 5.59 us
    pallas_call x1 -> x2, Pallas kernels: 19.3 us -> 20.4 us  [the longest x1 19.3 us: local(): pl.pallas_call(functools.partial(kernel, n, nd), out_shape=shapes, in_spe...]
where the time goes in v2:
time: 27.7 us; the launch traced here: 27.4 us
  Pallas kernels  20.4 us (74%)
  local copies, waits for them, and re-layouts  5.59 us (20%)
  between operations  1.34 us (5%)
    pallas_call x1, Pallas kernels, local(): pl.pallas_call(functools.partial(kernel, n, nd), out_shape=shapes, in_spe...  19.3 us
    unnamed x16, local copies, waits for them, and re-layouts  5.59 us
    pallas_call x1, Pallas kernels, local(): pl.pallas_call(put_out, out_shape=shapes, in_specs=[pl.BlockSpec(memory_s...  1.12 us

profile of v2, /device:TPU:0, one launch (start us, length us, event | category | flops | bytes accessed | tf_op | source)
XLA Modules:
  0.0 27.4 jit_solution(12854226960075738766)
XLA Ops:
  0.6 0.0 copy-start.4
  1.3 0.0 copy-start.6
  1.3 0.0 copy-start.7
  1.3 0.0 copy-done.4
  1.3 0.6 %copy-done.6 = f32[128]{0:T(128)S(1)} copy-done((f32[128]{0:T(128)S(1)}, f32[128]{0:T(128)}, u32[]{:S(2)}) %copy-start.6) | copy-done | bytes 536
  2.0 0.0 copy-done.7
  2.0 0.0 copy-start
  2.0 1.2 %copy-done = bf16[128,4096]{1,0:T(8,128)(2,1)S(1)} copy-done((bf16[128,4096]{1,0:T(8,128)(2,1)S(1)}, bf16[128,4096]{1,0:T(8,128)(2,1)}, u32[]{:S(2)}) %copy-start) | copy-done | bytes 1048600
  3.2 0.0 copy-start.1
  3.2 1.2 %copy-done.1 = bf16[128,4096]{1,0:T(8,128)(2,1)S(1)} copy-done((bf16[128,4096]{1,0:T(8,128)(2,1)S(1)}, bf16[128,4096]{1,0:T(8,128)(2,1)}, u32[]{:S(2)}) %copy-start.1) | copy-done | bytes 1048600
  4.4 0.0 copy-start.2
  4.4 0.9 %copy-done.2 = bf16[128,512]{1,0:T(8,128)(2,1)S(1)} copy-done((bf16[128,512]{1,0:T(8,128)(2,1)S(1)}, bf16[128,512]{1,0:T(8,128)(2,1)}, u32[]{:S(2)}) %copy-start.2) | copy-done | bytes 131096
  5.3 0.0 copy-start.3
  5.3 0.9 %copy-done.3 = bf16[128,512]{1,0:T(8,128)(2,1)S(1)} copy-done((bf16[128,512]{1,0:T(8,128)(2,1)S(1)}, bf16[128,512]{1,0:T(8,128)(2,1)}, u32[]{:S(2)}) %copy-start.3) | copy-done | bytes 131096
  6.2 0.0 copy-start.5
  6.2 0.7 %copy-done.5 = bf16[4,512]{1,0:T(4,128)(2,1)S(1)} copy-done((bf16[4,512]{1,0:T(4,128)(2,1)S(1)}, bf16[4,512]{1,0:T(4,128)(2,1)}, u32[]{:S(2)}) %copy-start.5) | copy-done | bytes 4120
  6.9 19.3 %gqa_back.1 = (bf16[128,4096]{1,0:T(8,128)(2,1)S(1)}, bf16[128,512]{1,0:T(8,128)(2,1)S(1)}, bf16[128,512]{1,0:T(8,128)(2,1)S(1)}, bf16[4,512]{1,0:T(4,128)(2,1)S...) custom-call(s32[1]{0:T(128)S(6)} %copy.16.len_hbm, bf16[128,4096]{1,0:T(8,128)(2,1)S(1)} %copy-done, ...), custom_call_target="tpu_custom_call" | custom-call | tf_op jit(solution)/shard_map/gqa_back/pallas_call | solution.py:301
  26.3 1.1 %put_out.1 = (bf16[128,4096]{1,0:T(8,128)(2,1)}, bf16[128,512]{1,0:T(8,128)(2,1)}, bf16[128,512]{1,0:T(8,128)(2,1)}, bf16[4,512]{1,0:T(4,128)(2,1)}, bf16[4,512]...) custom-call(bf16[128,4096]{1,0:T(8,128)(2,1)S(1)} %get-tuple-element.21.refs_0_, ...), custom_call_target="tpu_custom_call" | custom-call | tf_op jit(solution)/shard_map/put_out/pallas_call | solution.py:344
Async XLA Ops:
  0.6 0.7 %copy-start.4 = (bf16[4,512]{1,0:T(4,128)(2,1)S(1)}, bf16[4,512]{1,0:T(4,128)(2,1)}, u32[]{:S(2)}) copy-start(bf16[4,512]{1,0:T(4,128)(2,1)} %pk_hbm.1) | copy-start | bytes 12292
  1.3 0.7 %copy-start.6 = (f32[128]{0:T(128)S(1)}, f32[128]{0:T(128)}, u32[]{:S(2)}) copy-start(f32[128]{0:T(128)} %param.15) | copy-start | bytes 1540
  1.3 0.7 %copy-start.7 = (f32[128]{0:T(128)S(1)}, f32[128]{0:T(128)}, u32[]{:S(2)}) copy-start(f32[128]{0:T(128)} %param.16) | copy-start | bytes 1540
  2.0 1.2 %copy-start = (bf16[128,4096]{1,0:T(8,128)(2,1)S(1)}, bf16[128,4096]{1,0:T(8,128)(2,1)}, u32[]{:S(2)}) copy-start(bf16[128,4096]{1,0:T(8,128)(2,1)} %q_hbm.1) | copy-start | bytes 3145732
  3.2 1.2 %copy-start.1 = (bf16[128,4096]{1,0:T(8,128)(2,1)S(1)}, bf16[128,4096]{1,0:T(8,128)(2,1)}, u32[]{:S(2)}) copy-start(bf16[128,4096]{1,0:T(8,128)(2,1)} %do_hbm.1) | copy-start | bytes 3145732
  4.4 0.9 %copy-start.2 = (bf16[128,512]{1,0:T(8,128)(2,1)S(1)}, bf16[128,512]{1,0:T(8,128)(2,1)}, u32[]{:S(2)}) copy-start(bf16[128,512]{1,0:T(8,128)(2,1)} %ck_hbm.1) | copy-start | bytes 393220
  5.3 0.9 %copy-start.3 = (bf16[128,512]{1,0:T(8,128)(2,1)S(1)}, bf16[128,512]{1,0:T(8,128)(2,1)}, u32[]{:S(2)}) copy-start(bf16[128,512]{1,0:T(8,128)(2,1)} %cv_hbm.1) | copy-start | bytes 393220
  6.2 0.7 %copy-start.5 = (bf16[4,512]{1,0:T(4,128)(2,1)S(1)}, bf16[4,512]{1,0:T(4,128)(2,1)}, u32[]{:S(2)}) copy-start(bf16[4,512]{1,0:T(4,128)(2,1)} %pv_hbm.1) | copy-start | bytes 12292

commit v3 on v2

--- a/solution.py
+++ b/solution.py
@@ -339,8 +339,9 @@
         compiler_params=pltpu.CompilerParams(
             collective_id=0, has_side_effects=True, vmem_limit_bytes=48 * 1024 * 1024),
         name="gqa_back",
-    )(lengths, query, comp_key, comp_value, prompt_key, prompt_value, d_out,
-      q_gain.reshape(1, HD), k_gain.reshape(1, HD))
+    )(lengths, *(pltpu.with_memory_space_constraint(a, pltpu.HBM) for a in (
+        query, comp_key, comp_value, prompt_key, prompt_value, d_out,
+        q_gain.reshape(1, HD), k_gain.reshape(1, HD))))
     res = pl.pallas_call(
         put_out,
         out_shape=shapes,

time: 27.7 us -> 22.1 us (0.80)
  local copies, waits for them, and re-layouts: 5.59 us -> 0 us
  Pallas kernels: 20.4 us -> 20.7 us
    unnamed x16 -> x0, local copies, waits for them, and re-layouts: 5.59 us -> none
where the time goes in v3:
time: 22.1 us; the launch traced here: 22 us
  Pallas kernels  20.7 us (94%)
  between operations  1.29 us (6%)
    pallas_call x1, Pallas kernels, local(): pl.pallas_call(functools.partial(kernel, n, nd), out_shape=shapes, in_spe...  19.6 us
    pallas_call x1, Pallas kernels, local(): pl.pallas_call(put_out, out_shape=shapes, in_specs=[pl.BlockSpec(memory_s...  1.12 us

profile of v3, /device:TPU:0, one launch (start us, length us, event | category | flops | bytes accessed | tf_op | source)
XLA Modules:
  0.0 22.0 jit_solution(7090171759745138199)
XLA Ops:
  1.3 19.6 %gqa_back.1 = (bf16[128,4096]{1,0:T(8,128)(2,1)S(1)}, bf16[128,512]{1,0:T(8,128)(2,1)S(1)}, bf16[128,512]{1,0:T(8,128)(2,1)S(1)}, bf16[4,512]{1,0:T(4,128)(2,1)S...) custom-call(s32[1]{0:T(128)S(6)} %copy.16.len_hbm, bf16[128,4096]{1,0:T(8,128)(2,1)} %q_hbm.1, ...), custom_call_target="tpu_custom_call" | custom-call | tf_op jit(solution)/shard_map/gqa_back/pallas_call | solution.py:301
  20.8 1.1 %put_out.1 = (bf16[128,4096]{1,0:T(8,128)(2,1)}, bf16[128,512]{1,0:T(8,128)(2,1)}, bf16[128,512]{1,0:T(8,128)(2,1)}, bf16[4,512]{1,0:T(4,128)(2,1)}, bf16[4,512]...) custom-call(bf16[128,4096]{1,0:T(8,128)(2,1)S(1)} %get-tuple-element.21.refs_0_, ...), custom_call_target="tpu_custom_call" | custom-call | tf_op jit(solution)/shard_map/put_out/pallas_call | solution.py:345

commit v4 on v3

--- a/solution.py
+++ b/solution.py
@@ -33,7 +33,7 @@
     len_hbm, q_hbm, ck_hbm, cv_hbm, pk_hbm, pv_hbm, do_hbm, qg_hbm, kg_hbm,
     dqv, dckv, dcvv, dpkv, dpvv, gq_ref, gk_ref,
     len_ref, qg_ref, kg_ref,
-    qv, dov, ckv, vv, pkb, pvb, pf, pvf, uu, kgs, ss, dd, ee, rss, tots, dss, cs, ws, dvs,
+    qv, dov, ckv, vv, pkb, pvb, pf, pvf, uu, kgs, dd, ee, sums, pws, dss, cs, ws, dvs,
     stg, share, rbuf, gbuf, hbuf,
     q_sem, do_sem, in_sem, pks, pkr, pvs, pvr, shs, shr, gs, gr, hs, hr,
 ):
@@ -76,12 +76,14 @@
         q_in[g].start()
         do_in[g].start()
 
+    ins[2].wait()
+    ins[3].wait()
     pl.semaphore_wait(barrier, n - 1 + nd - 1)
     gathers = []
     for k in range(1, n):
-        for src, buf, ssem, rsem in ((pk_hbm, pkb, pks, pkr), (pv_hbm, pvb, pvs, pvr)):
+        for buf, ssem, rsem in ((pkb, pks, pkr), (pvb, pvs, pvr)):
             c = pltpu.make_async_remote_copy(
-                src_ref=src, dst_ref=buf.at[k], send_sem=ssem.at[k - 1], recv_sem=rsem.at[k - 1],
+                src_ref=buf.at[0], dst_ref=buf.at[k], send_sem=ssem.at[k - 1], recv_sem=rsem.at[k - 1],
                 device_id=peer(k), device_id_type=MESH)
             c.start()
             gathers.append(c)
@@ -105,8 +107,6 @@
     krow = lax.broadcasted_iota(jnp.int32, (count, 2 * HD), 0)
     qcol = lax.broadcasted_iota(jnp.int32, (count, 2 * HD), 1)
     seen = krow <= jnp.where(qcol >= HD, qcol - HD, qcol)
-    live = qcol[0:1]
-    live = jnp.where(live >= HD, live - HD, live) < len_ref[0]
     ones = jnp.ones((8, HD), BF16)
 
     def pair(ref, c0):
@@ -127,15 +127,16 @@
             s = dot_nt(kgs[plen:total, hc], x)
             d = dot_nt(vv[plen:total, hc], go)
             e = jnp.where(seen, jnp.exp2(s * (rs * LOG2E)), 0.0)
-            ss[:, cc] = s
-            dd[:, cc] = d
-            ee[:, cc] = e
-            rss[0:1, cc] = r
-            tots[0:1, cc] = jnp.sum(e, axis=0, keepdims=True)
-            tots[1:2, cc] = jnp.sum(e * d, axis=0, keepdims=True)
-
-    ins[2].wait()
-    ins[3].wait()
+            d = d * rs
+            ed = e * d
+            ee[:, cc] = e.astype(BF16)
+            dd[:, cc] = d.astype(BF16)
+            sums[0:1, cc] = r
+            sums[1:2, cc] = jnp.sum(e, axis=0, keepdims=True)
+            sums[2:3, cc] = jnp.sum(ed, axis=0, keepdims=True)
+            sums[3:4, cc] = jnp.sum(e * s, axis=0, keepdims=True)
+            sums[4:5, cc] = jnp.sum(ed * s, axis=0, keepdims=True)
+
     for c in gathers:
         c.wait_recv()
     for k in range(n):
@@ -149,41 +150,49 @@
         kgs[0:plen, hc] = (u * gain).astype(BF16)
     vv[0:plen, :] = pvf[...].astype(BF16)
 
+    def heads(ref, g):
+        return jnp.concatenate(
+            [ref[:, g * width + i * HD:g * width + (i + 1) * HD] for i in range(GROUPS)], axis=0)
+
+    slot = lax.rem(lax.broadcasted_iota(jnp.int32, (1, width), 1), HD)
+    live = slot < len_ref[0]
+    for g in range(HK):
+        hc = slice(g * HD, (g + 1) * HD)
+        gc = slice(g * width, (g + 1) * width)
+        r = sums[0:1, gc]
+        rs = r * SCALE
+        sp = dot_nt(kgs[0:plen, hc], heads(qv, g))
+        dpr = dot_nt(vv[0:plen, hc], heads(dov, g)) * rs
+        ep = jnp.exp2(sp * (rs * LOG2E))
+        ed = ep * dpr
+        tot = sums[1:2, gc] + jnp.sum(ep, axis=0, keepdims=True)
+        t2 = sums[2:3, gc] + jnp.sum(ed, axis=0, keepdims=True)
+        m1 = sums[3:4, gc] + jnp.sum(ep * sp, axis=0, keepdims=True)
+        m2 = sums[4:5, gc] + jnp.sum(ed * sp, axis=0, keepdims=True)
+        inv = 1.0 / tot
+        delta = t2 * inv
+        inv = jnp.where(live, inv, 0.0)
+        c = r * r * inv * (m2 - delta * m1) * (1.0 / HD)
+        for i in range(GROUPS):
+            cs[g * GROUPS + i:g * GROUPS + i + 1, :] = c[:, i * HD:(i + 1) * HD]
+        pp = ep * inv
+        pws[0:plen, gc] = pp.astype(BF16)
+        dss[0:plen, gc] = (pp * (dpr - delta)).astype(BF16)
+        sums[5:6, gc] = inv
+        sums[6:7, gc] = delta
+
     tsum = jnp.zeros((1, HD), F32)
     for g in range(HK):
         hc = slice(g * HD, (g + 1) * HD)
-        w = jnp.zeros((total, HD), F32)
-        dv = jnp.zeros((total, HD), F32)
-        for j in range(GROUPS // 2):
-            c0 = g * width + j * 2 * HD
-            cc = slice(c0, c0 + 2 * HD)
-            x = pair(qv, c0)
-            go = pair(dov, c0)
-            r = rss[0:1, cc]
-            rs = r * SCALE
-            sp = dot_nt(kgs[0:plen, hc], x)
-            dpr = dot_nt(vv[0:plen, hc], go)
-            ep = jnp.exp2(sp * (rs * LOG2E))
-            tot = tots[0:1, cc] + jnp.sum(ep, axis=0, keepdims=True)
-            t2 = tots[1:2, cc] + jnp.sum(ep * dpr, axis=0, keepdims=True)
-            inv = 1.0 / tot
-            delta = t2 * inv
-            inv = jnp.where(live, inv, 0.0)
-            pp = ep * inv
-            dsp = pp * ((dpr - delta) * rs)
-            pc = ee[:, cc] * inv
-            dsc = pc * ((dd[:, cc] - delta) * rs)
-            m = (jnp.sum(dsp * sp, axis=0, keepdims=True)
-                 + jnp.sum(dsc * ss[:, cc], axis=0, keepdims=True))
-            c = r * r * m * (1.0 / HD)
-            hh = g * GROUPS + 2 * j
-            cs[hh:hh + 1, :] = c[:, 0:HD]
-            cs[hh + 1:hh + 2, :] = c[:, HD:2 * HD]
-            pw = jnp.concatenate([pp.astype(BF16), pc.astype(BF16)], axis=0)
-            ds = jnp.concatenate([dsp.astype(BF16), dsc.astype(BF16)], axis=0)
-            dss[:, cc] = ds
-            w = w + jnp.dot(ds, x, preferred_element_type=F32)
-            dv = dv + jnp.dot(pw, go, preferred_element_type=F32)
+        gc = slice(g * width, (g + 1) * width)
+        inv = jnp.broadcast_to(sums[5:6, gc], (16, width)).astype(BF16)[None]
+        delta = jnp.broadcast_to(sums[6:7, gc], (16, width)).astype(BF16)[None]
+        pc = ee[:, gc].reshape(count // 16, 16, width) * inv
+        dsc = pc * (dd[:, gc].reshape(count // 16, 16, width) - delta)
+        pws[plen:total, gc] = pc.reshape(count, width)
+        dss[plen:total, gc] = dsc.reshape(count, width)
+        w = jnp.dot(dss[:, gc], heads(qv, g), preferred_element_type=F32)
+        dv = jnp.dot(pws[:, gc], heads(dov, g), preferred_element_type=F32)
         ws[:, hc] = w
         dvs[:, hc] = dv
         tsum = tsum + jnp.sum(w * uu[:, hc], axis=0, keepdims=True)
@@ -270,9 +279,15 @@
         c.wait_send()
 
 
+CUTS = 8
+
+
 def put_out(*refs):
     sem = refs[14]
-    copies = [pltpu.make_async_copy(refs[i], refs[7 + i], sem.at[i]) for i in range(7)]
+    rows = refs[0].shape[0] // CUTS
+    parts = [(refs[0].at[pl.ds(i * rows, rows)], refs[7].at[pl.ds(i * rows, rows)]) for i in range(CUTS)]
+    parts += list(zip(refs[1:7], refs[8:14]))
+    copies = [pltpu.make_async_copy(a, b, sem.at[i]) for i, (a, b) in enumerate(parts)]
     for c in copies:
         c.start()
     for c in copies:
@@ -317,11 +332,10 @@
             pltpu.VMEM((plen, wk), F32),
             pltpu.VMEM((total, wk), F32),
             pltpu.VMEM((total, wk), BF16),
-            pltpu.VMEM((count, wq), F32),
-            pltpu.VMEM((count, wq), F32),
-            pltpu.VMEM((count, wq), F32),
+            pltpu.VMEM((count, wq), BF16),
+            pltpu.VMEM((count, wq), BF16),
             pltpu.VMEM((8, wq), F32),
-            pltpu.VMEM((8, wq), F32),
+            pltpu.VMEM((total, wq), BF16),
             pltpu.VMEM((total, wq), BF16),
             pltpu.VMEM((HQ, HD), F32),
             pltpu.VMEM((total, wk), F32),
@@ -347,7 +361,7 @@
         out_shape=shapes,
         in_specs=[pl.BlockSpec(memory_space=pl.ANY)] * 7,
         out_specs=[hbm] * 7,
-        scratch_shapes=[dma((7,))],
+        scratch_shapes=[dma((6 + CUTS,))],
         compiler_params=pltpu.CompilerParams(vmem_limit_bytes=1024 * 1024),
         name="put_out",
     )(*res)

time: 22.1 us -> 20.7 us (0.937)
  Pallas kernels: 20.7 us -> 19.2 us
    pallas_call x1, Pallas kernels: 19.6 us -> 18.1 us  [local(): pl.pallas_call(functools.partial(kernel, n, nd), out_shape=shapes, in_spe...]
where the time goes in v4:
time: 20.7 us; the launch traced here: 20.5 us
  Pallas kernels  19.2 us (93%)
  between operations  1.29 us (6%)
    pallas_call x1, Pallas kernels, local(): pl.pallas_call(functools.partial(kernel, n, nd), out_shape=shapes, in_spe...  18.1 us
    pallas_call x1, Pallas kernels, local(): pl.pallas_call(put_out, out_shape=shapes, in_specs=[pl.BlockSpec(memory_s...  1.18 us

profile of v4, /device:TPU:0, one launch (start us, length us, event | category | flops | bytes accessed | tf_op | source)
XLA Modules:
  0.0 20.5 jit_solution(4969397261707947307)
XLA Ops:
  1.3 18.1 %gqa_back.1 = (bf16[128,4096]{1,0:T(8,128)(2,1)S(1)}, bf16[128,512]{1,0:T(8,128)(2,1)S(1)}, bf16[128,512]{1,0:T(8,128)(2,1)S(1)}, bf16[4,512]{1,0:T(4,128)(2,1)S...) custom-call(s32[1]{0:T(128)S(6)} %copy.16.len_hbm, bf16[128,4096]{1,0:T(8,128)(2,1)} %q_hbm.1, ...), custom_call_target="tpu_custom_call" | custom-call | tf_op jit(solution)/shard_map/gqa_back/pallas_call | solution.py:316
  19.4 1.2 %put_out.1 = (bf16[128,4096]{1,0:T(8,128)(2,1)}, bf16[128,512]{1,0:T(8,128)(2,1)}, bf16[128,512]{1,0:T(8,128)(2,1)}, bf16[4,512]{1,0:T(4,128)(2,1)}, bf16[4,512]...) custom-call(bf16[128,4096]{1,0:T(8,128)(2,1)S(1)} %get-tuple-element.21.refs_0_, ...), custom_call_target="tpu_custom_call" | custom-call | tf_op jit(solution)/shard_map/put_out/pallas_call | solution.py:359
